TPU v7x, 32 devices: a whole 2x2x4 slice. The times are simulated.
32 devices in a mesh: img: 8 (over z, y), band: 4 (over x, core).
Axes of the slice: x: 2, y: 2, z: 4, core: 2. Of those that a mesh axis runs over, the one named last changes fastest.
Arguments:
- patches: bfloat16 [32, 576, 768], P('img', 'band'), may hold values from -6 to 6
- patch_mask: int32 [32, 576], P('img', 'band'), may hold values from 0 to 1, as said below
- band_first: int32 [32, 4], P('img'), may hold values from 0 to 18, as said below
- attn_gain: bfloat16 [768], replicated, may hold values from 0.5 to 1.5
- attn_shift: bfloat16 [768], replicated, may hold values from -3 to 3
- inproj_weight: bfloat16 [768, 2304], replicated, may hold values from -0.21875 to 0.21875
- inproj_bias: bfloat16 [2304], replicated, may hold values from -2 to 2
- rotary_freqs: bfloat16 [2, 12, 32], replicated, may hold values from -3 to 3
- outproj_weight: bfloat16 [768, 768], replicated, may hold values from -0.875 to 0.875
- outproj_bias: bfloat16 [768], replicated, may hold values from -2 to 2
- mlp_gain: bfloat16 [768], replicated, may hold values from 0.5 to 1.5
- mlp_shift: bfloat16 [768], replicated, may hold values from -3 to 3
- expand_weight: bfloat16 [768, 3072], replicated, may hold values from -0.21875 to 0.21875
- expand_bias: bfloat16 [3072], replicated, may hold values from -2 to 2
- reduce_weight: bfloat16 [3072, 768], replicated, may hold values from -0.109375 to 0.109375
- reduce_bias: bfloat16 [768], replicated, may hold values from -2 to 2
- cotangent: bfloat16 [32, 576, 768], P('img', 'band'), may hold values from -6 to 6
Outputs:
- block_out: bfloat16 [32, 576, 768], P('img', 'band')
- d_patches: bfloat16 [32, 576, 768], P('img', 'band')
- grad_attn_gain: float32 [768], P('img')
- grad_attn_shift: float32 [768], P('img')
- grad_inproj_weight: float32 [768, 2304], P('img')
- grad_inproj_bias: float32 [2304], P('img')
- grad_rotary_freqs: float32 [2, 12, 32], replicated
- grad_outproj_weight: float32 [768, 768], P('img')
- grad_outproj_bias: float32 [768], P('img')
- grad_mlp_gain: float32 [768], P('img')
- grad_mlp_shift: float32 [768], P('img')
- grad_expand_weight: float32 [768, 3072], P('img')
- grad_expand_bias: float32 [3072], P('img')
- grad_reduce_weight: float32 [3072, 768], P('img')
- grad_reduce_bias: float32 [768], P('img')
Inputs may be any that keep to these rules, and one draw needn't show every extreme that they name: `patch_mask`: each image has a square grid of side 24 * 7 // 12, 20 or 24, and image 0 has side 24; the grid's rows are split over the 4 bands as evenly as possible, earlier bands taking one row more; a slot of local row i and column j of band b is 1 exactly when i is under the band's row count and j under the side. `band_first`: the first patch row of each band of each image, consistent with patch_mask's row counts.
All inputs are finite; a program needn't handle non-finite values.
Results may differ from a plain program's by a relative error of at most 0.012.
The roundings to bfloat16 on the way count: a program that leaves them out, or rounds other values in their place, can miss the bound.
Values may be sent and summed in bfloat16 or wider, within the bound.
No kernel may reach another device: no remote copies, remote signals or barrier semaphores. Data moves between devices by JAX's collectives and lax.ppermute only.
A program may use at most 192 MiB of HBM per device.

v0:
```python
import jax
import jax.numpy as jnp
from jax import lax
from jax.sharding import PartitionSpec as P

GRID = 24
EPS = 1e-06
NEG = -1e30


def norm_parts(values):
    center = values - jnp.mean(values, -1, keepdims=True)
    rstd = lax.rsqrt(jnp.mean(center * center, -1, keepdims=True) + EPS)
    return (center * rstd, rstd)


def norm_back(grad, gain, xhat, rstd):
    scaled = grad * gain
    inner = jnp.mean(scaled * xhat, -1, keepdims=True)
    return rstd * (scaled - jnp.mean(scaled, -1, keepdims=True) - xhat * inner)


def turn(tensor, cosine, sine):
    half = tensor.shape[-1] // 2
    first, second = (tensor[..., :half], tensor[..., half:])
    return jnp.concatenate([first * cosine - second * sine, first * sine + second * cosine], -1)


def matrix_sum(grad):
    low = grad.astype(jnp.bfloat16)
    low = lax.psum_scatter(low, "band", scatter_dimension=1, tiled=True)
    low = lax.psum_scatter(low, "img", scatter_dimension=0, tiled=True)
    low = lax.all_gather(low, "band", axis=1, tiled=True)
    return low.astype(jnp.float32)


def local(
    patches,
    patch_mask,
    band_first,
    attn_gain,
    attn_shift,
    inproj_weight,
    inproj_bias,
    rotary_freqs,
    outproj_weight,
    outproj_bias,
    mlp_gain,
    mlp_shift,
    expand_weight,
    expand_bias,
    reduce_weight,
    reduce_bias,
    cotangent,
):
    single = jnp.float32
    low = jnp.bfloat16
    images, slots, width = patches.shape
    heads = rotary_freqs.shape[1]
    size = width // heads
    scale = size ** (-0.5)
    bands = lax.axis_size("band")
    here = lax.axis_index("band")

    def gather_image(values):
        return lax.all_to_all(values, "band", 0, 1, tiled=True)

    def spread_image(values):
        return lax.all_to_all(values, "band", 1, 0, tiled=True)

    patches = gather_image(patches)
    cotangent = gather_image(cotangent)
    mask = gather_image(patch_mask).astype(single)
    count = images // bands
    total = slots * bands
    starts = lax.dynamic_slice_in_dim(band_first, here * count, count, 0)
    row_in = jnp.arange(slots) // GRID
    rows = (starts[:, :, None] + row_in[None, None, :]).reshape(count, total).astype(single)
    cols = jnp.broadcast_to((jnp.arange(total) % GRID).astype(single)[None, :], rows.shape)
    freqs = rotary_freqs.astype(single)
    angles = rows[..., None, None] * freqs[0] + cols[..., None, None] * freqs[1]
    cosine, sine = (jnp.cos(angles), jnp.sin(angles))
    wide = patches.astype(single)
    xhat_one, rstd_one = norm_parts(wide)
    gain_one = attn_gain.astype(single)
    attn_in = (xhat_one * gain_one + attn_shift.astype(single)).astype(low)
    projected = jnp.dot(attn_in, inproj_weight, preferred_element_type=single)
    projected = projected + inproj_bias.astype(single)
    split = projected.reshape(count, total, 3, heads, size)
    query_rot = turn(split[:, :, 0], cosine, sine).astype(low)
    key_rot = turn(split[:, :, 1], cosine, sine).astype(low)
    value_low = split[:, :, 2].astype(low)
    scores = jnp.einsum("iqhd,ikhd->ihqk", query_rot, key_rot, preferred_element_type=single)
    masked = jnp.where(mask[:, None, None, :] > 0, scores * scale, NEG)
    expo = jnp.exp(masked - jnp.max(masked, -1, keepdims=True))
    probs = expo / jnp.sum(expo, -1, keepdims=True)
    probs_low = probs.astype(low)
    mix = jnp.einsum("ihqk,ikhd->iqhd", probs_low, value_low, preferred_element_type=single)
    mix = mix.reshape(count, total, width).astype(low)
    attn_out = jnp.dot(mix, outproj_weight, preferred_element_type=single)
    resid_mid = wide + attn_out + outproj_bias.astype(single)
    xhat_two, rstd_two = norm_parts(resid_mid)
    gain_two = mlp_gain.astype(single)
    mlp_in = (xhat_two * gain_two + mlp_shift.astype(single)).astype(low)
    pre_act = jnp.dot(mlp_in, expand_weight, preferred_element_type=single)
    pre_act = pre_act + expand_bias.astype(single)
    half_erf = 0.5 + 0.5 * lax.erf(pre_act * 0.5**0.5)
    hidden = (pre_act * half_erf).astype(low)
    slope = half_erf + pre_act * jnp.exp(-0.5 * pre_act * pre_act) * 0.3989422804014327
    branch = jnp.dot(hidden, reduce_weight, preferred_element_type=single)
    block_out = mask[..., None] * (resid_mid + branch + reduce_bias.astype(single))
    block_out = spread_image(block_out.astype(low))
    grad_top = cotangent.astype(single) * mask[..., None]
    grad_low = grad_top.astype(low)
    grad_reduce_weight = jnp.einsum("iqf,iqd->fd", hidden, grad_low, preferred_element_type=single)
    grad_reduce_bias = jnp.sum(grad_top, (0, 1))
    d_hidden = jnp.einsum("iqd,fd->iqf", grad_low, reduce_weight, preferred_element_type=single)
    d_pre = (d_hidden * slope).astype(low)
    grad_expand_weight = jnp.einsum("iqd,iqf->df", mlp_in, d_pre, preferred_element_type=single)
    grad_expand_bias = jnp.sum(d_pre.astype(single), (0, 1))
    d_mlp_in = jnp.einsum("iqf,df->iqd", d_pre, expand_weight, preferred_element_type=single)
    grad_mlp_gain = jnp.sum(d_mlp_in * xhat_two, (0, 1))
    grad_mlp_shift = jnp.sum(d_mlp_in, (0, 1))
    d_mid = grad_top + norm_back(d_mlp_in, gain_two, xhat_two, rstd_two)
    d_attn = d_mid.astype(low)
    grad_outproj_weight = jnp.einsum("iqe,iqd->ed", mix, d_attn, preferred_element_type=single)
    grad_outproj_bias = jnp.sum(d_attn.astype(single), (0, 1))
    d_mix = jnp.einsum("iqd,ed->iqe", d_attn, outproj_weight, preferred_element_type=single)
    d_mix = d_mix.astype(low).reshape(count, total, heads, size)
    d_values = jnp.einsum("ihqk,iqhd->ikhd", probs_low, d_mix, preferred_element_type=single)
    d_probs = jnp.einsum("iqhd,ikhd->ihqk", d_mix, value_low, preferred_element_type=single)
    inner = jnp.sum(probs * d_probs, -1, keepdims=True)
    d_scores = (probs * (d_probs - inner)).astype(low)
    d_qrot = scale * jnp.einsum("ihqk,ikhd->iqhd", d_scores, key_rot, preferred_element_type=single)
    d_krot = scale * jnp.einsum(
        "ihqk,iqhd->ikhd", d_scores, query_rot, preferred_element_type=single
    )
    half = size // 2
    slope_q = (
        d_qrot[..., half:] * query_rot[..., :half] - d_qrot[..., :half] * query_rot[..., half:]
    )
    slope_k = d_krot[..., half:] * key_rot[..., :half] - d_krot[..., :half] * key_rot[..., half:]
    d_angle = slope_q + slope_k
    grad_freqs = jnp.stack(
        [
            jnp.sum(rows[..., None, None] * d_angle, (0, 1)),
            jnp.sum(cols[..., None, None] * d_angle, (0, 1)),
        ]
    )
    d_queries = turn(d_qrot, cosine, -sine)
    d_keys = turn(d_krot, cosine, -sine)
    flat = (count, total, width)
    d_proj = jnp.concatenate(
        [d_queries.reshape(flat), d_keys.reshape(flat), d_values.reshape(flat)], -1
    ).astype(low)
    grad_inproj_weight = jnp.einsum("iqd,iqe->de", attn_in, d_proj, preferred_element_type=single)
    grad_inproj_bias = jnp.sum(d_proj.astype(single), (0, 1))
    d_attn_in = jnp.einsum("iqe,de->iqd", d_proj, inproj_weight, preferred_element_type=single)
    grad_attn_gain = jnp.sum(d_attn_in * xhat_one, (0, 1))
    grad_attn_shift = jnp.sum(d_attn_in, (0, 1))
    d_patches = d_mid + norm_back(d_attn_in, gain_one, xhat_one, rstd_one)
    d_patches = spread_image(d_patches.astype(low))
    small = (
        grad_attn_gain,
        grad_attn_shift,
        grad_inproj_bias,
        grad_outproj_bias,
        grad_mlp_gain,
        grad_mlp_shift,
        grad_expand_bias,
        grad_reduce_bias,
        grad_freqs.reshape(-1),
    )
    packed = lax.psum(jnp.concatenate(small), ("img", "band"))
    shares = lax.axis_size("img")
    mine = lax.axis_index("img")
    sums = []
    at = 0
    for piece in small:
        long = piece.shape[0]
        sums.append(packed[at : at + long])
        at += long
    freq_total = sums.pop().reshape(grad_freqs.shape)
    sums = [
        lax.dynamic_slice_in_dim(s, mine * (s.shape[0] // shares), s.shape[0] // shares)
        for s in sums
    ]
    return (
        block_out,
        d_patches,
        sums[0],
        sums[1],
        matrix_sum(grad_inproj_weight),
        sums[2],
        freq_total,
        matrix_sum(grad_outproj_weight),
        sums[3],
        sums[4],
        sums[5],
        matrix_sum(grad_expand_weight),
        sums[6],
        matrix_sum(grad_reduce_weight),
        sums[7],
    )


def solution(mesh):
    act = P("img", "band", None)
    row = P("img")
    mat = P("img", None)
    return jax.shard_map(
        local,
        mesh=mesh,
        in_specs=(act, P("img", "band"), P("img", None)) + (P(),) * 13 + (act,),
        out_specs=(act, act, row, row, mat, row, P(), mat, row, row, row, mat, row, mat, row),
        check_vma=False,
    )
```

profile of v0, /device:TPU:0, one launch (start us, length us, event | category | flops | bytes accessed | tf_op | source)
XLA Modules:
  0.0 651.7 jit_solution(12072034389343736507)
XLA Ops:
  8.6 4.2 all-to-all-start
  16.7 4.2 all-to-all-start.1
  33.7 4.2 all-to-all-start.3
  45.8 4.6 convolution_add_fusion
  50.3 6.5 copy.68
  56.9 2.4 slice_bitcast_fusion.1
  59.3 4.8 subtract_convert_fusion.1
  65.4 7.4 %fusion.34 = f32[12,576,576]{1,2,0:T(8,128)} fusion(bf16[576,12,32]{0,2,1:T(8,128)(2,1)S(1)} %bitcast.128, bf16[576,12,32]{0,2,1:T(8,128)(2,1)S(1)} %bitcast.130, bf16[576,12,32]{0,2,1:T(8,128)(2,1)S(1)} %bitcast.126, bf16[576,12,32]{0,2,1:T(8,128)(2,1)S(1)} %bitcast.124), kind=kOutput, calls=%fused_computation.88 | convolution fusion | flops 513146880 | bytes 17694720 | tf_op jit(solution)/shard_map/iqhd,ikhd->ihqk/dot_general | solution.py:93
  72.7 22.2 %fusion.54 = (f32[12,576]{1,0:T(8,128)}, f32[12,576,576]{1,2,0:T(8,128)}) fusion(f32[12,576,576]{1,2,0:T(8,128)} %fusion.34, pred[576]{0:T(1024)(128)(4,1)} %broadcast_compare_fusion), kind=kOutput, calls=%fused_computation.138 | output fusion | flops 23888448 | bytes 31878720 | tf_op jit(solution)/shard_map/sub | solution.py:95
  94.9 8.4 %fusion.21 = bf16[12,64,576]{2,1,0:T(8,128)(2,1)S(1)} fusion(f32[1,576,3,12,64]{1,4,3,2,0:T(8,128)} %bitcast.122, f32[12,576,576]{1,2,0:T(8,128)} %get-tuple-element.113, f32[12,576]{1,0:T(8,128)} %get-tuple-element.112), kind=kOutput, calls=%fused_computation.63 | convolution fusion | flops 518012928 | bytes 19603456 | tf_op jit(solution)/shard_map/ihqk,ikhd->iqhd/dot_general | solution.py:98
  104.2 3.3 fusion.20
  107.5 2.2 reduce_sum.183
  110.4 1.8 multiply_reduce_fusion.5
  112.8 8.9 %multiply_convert_fusion.1 = (bf16[576,3072]{1,0:T(8,128)(2,1)}, f32[576,3072]{1,0:T(8,128)}) fusion(f32[3072]{0:T(1024)} %convert_element_type.313, bf16[768,3072]{1,0:T(8,128)(2,1)} %param.29, f32[576,768]{1,0:T(8,128)} %fusion.20, f32[768]{0:T(1024)} %convert_element_type.311, f32[768]{0:T(1024)} %convert_element_type.310, f32[576]{0:T(1024)S(1)} %add_rsqrt_fusion, ...), kind=kOutput, calls=%fused_computation.18 | convolution fusion | flops 2730737664 | bytes 17127936 | tf_op jit(solution)/shard_map/dot_general | solution.py:105
  123.2 9.2 %convert_reduce_fusion = (f32[3072]{0:T(1024)}, bf16[576,3072]{1,0:T(8,128)(2,1)S(1)}) fusion(f32[576,3072]{1,0:T(8,128)} %get-tuple-element.115, f32[3072]{0:T(1024)} %convert_element_type.313, bf16[576,768]{1,0:T(8,128)(2,1)S(1)} %fusion.19, bf16[3072,768]{1,0:T(8,128)(2,1)} %param.31), kind=kOutput, calls=%fused_computation.17 | convolution fusion | flops 2740909056 | bytes 16244736 | tf_op jit(solution)/shard_map/iqd,fd->iqf/dot_general | solution.py:117
  132.4 7.6 %multiply_reduce_fusion.1 = (f32[768]{0:T(1024)}, f32[576]{0:T(1024)S(1)}, f32[576]{0:T(1024)S(1)}, f32[768]{0:T(1024)}, f32[576,768]{1,0:T(8,128)S(1)}) fusion(f32[576,768]{1,0:T(8,128)S(1)} %copy-done.1, f32[576]{0:T(1024)S(1)} %copy-done.40, f32[576]{0:T(1024)S(1)} %copy-done.32, f32[768]{0:T(1024)S(1)} %copy-done.37, ...), kind=kOutput, calls=%fused_computation.46 | convolution fusion | flops 2721887744 | bytes 11814912 | tf_op jit(solution)/shard_map/iqf,df->iqd/dot_general | solution.py:121
  140.0 2.6 convert_reduce_fusion.2
  143.8 2.2 convolution_convert_fusion.3
  146.0 3.6 convolution_convert_fusion.4
  149.6 2.2 copy.72
  151.8 15.5 %multiply_reduce_fusion = (f32[12,576]{1,0:T(8,128)S(1)}, f32[12,576,576]{1,2,0:T(8,128)}) fusion(f32[12,576,576]{1,2,0:T(8,128)} %get-tuple-element.113, f32[12,576]{1,0:T(8,128)} %get-tuple-element.112, bf16[576,12,64]{0,2,1:T(8,128)(2,1)} %bitcast.144, f32[1,576,3,12,64]{1,4,3,2,0:T(8,128)} %bitcast.123), kind=kOutput, calls=%fused_computation.2 | convolution fusion | flops 521544960 | bytes 35654656 | tf_op jit(solution)/shard_map/iqhd,ikhd->ihqk/dot_general | solution.py:131
  167.3 12.5 %multiply_convert_fusion = bf16[12,576,576]{1,2,0:T(8,128)(2,1)S(1)} fusion(f32[12,576,576]{1,2,0:T(8,128)} %get-tuple-element.118, f32[12,576]{1,0:T(8,128)S(1)} %get-tuple-element.117, f32[12,576,576]{1,2,0:T(8,128)} %get-tuple-element.113, f32[12,576]{1,0:T(8,128)S(1)} %copy-done.27), kind=kLoop, calls=%fused_computation.1 | loop fusion | flops 15925248 | bytes 39868416 | tf_op jit(solution)/shard_map/convert_element_type | solution.py:133
  179.9 4.0 multiply_bitcast_fusion
  183.9 3.0 multiply_bitcast_fusion.1
  186.9 6.6 %multiply_subtract_fusion.1 = (bf16[1,576,12,32]{1,3,2,0:T(8,128)(2,1)S(1)}, bf16[1,576,12,32]{1,3,2,0:T(8,128)(2,1)S(1)}, bf16[1,576,12,32]{1,3,2,0:T(8,128)(2,1)S(1)}, bf16[1,576,12,32]{1,3,2,0:T(8,128)(2,1)S(1)}) fusion(f32[1,576,12,64]{1,3,2,0:T(8,128)} %multiply_bitcast_fusion.1, f32[12,32]{1,0:T(8,128)} %get-tuple-element.111, f32[576]{0:T(1024)S(1)} %copy-done.24, ...), kind=kLoop, calls=%fused_computation.78 | loop fusion | flops 4423680 | bytes 5316096 | tf_op jit(solution)/shard_map/sub | solution.py:26
  195.1 9.5 %fusion.24 = bf16[12,64,576]{2,1,0:T(8,128)(2,1)S(1)} fusion(bf16[576,12,64]{0,2,1:T(8,128)(2,1)S(1)} %bitcast.145, f32[12,576,576]{1,2,0:T(8,128)} %get-tuple-element.113, f32[12,576]{1,0:T(8,128)S(1)} %copy-done.28), kind=kOutput, calls=%fused_computation.64 | convolution fusion | flops 518012928 | bytes 17722368 | tf_op jit(solution)/shard_map/ihqk,iqhd->ikhd/dot_general | solution.py:130
  205.6 7.2 %convolution_convert_fusion = bf16[768,2304]{0,1:T(8,128)(2,1)} fusion(bf16[576,768]{0,1:T(8,128)(2,1)S(1)} %bitcast.146, bf16[576,768]{0,1:T(8,128)(2,1)S(1)} %bitcast.141, bf16[576,768]{0,1:T(8,128)(2,1)S(1)} %bitcast.138, f32[576,768]{1,0:T(8,128)S(1)} %copy-done.16, f32[768]{0:T(1024)S(1)} %copy-done.43, f32[768]{0:T(1024)S(1)} %copy-done.35), kind=kOutput, calls=%fused_computation.21 | convolution fusion | flops 2049490944 | bytes 7968768 | tf_op jit(solution)/shard_map/iqd,iqe->de/dot_general | solution.py:156
  213.0 8.3 %convolution_convert_fusion.1 = bf16[3072,768]{0,1:T(8,128)(2,1)} fusion(bf16[576,3072]{1,0:T(8,128)(2,1)} %get-tuple-element.114, bf16[576,768]{1,0:T(8,128)(2,1)} %copy-done.20), kind=kOutput, calls=%fused_computation.22 | convolution fusion | flops 2720268288 | bytes 9142272 | tf_op jit(solution)/shard_map/iqf,iqd->fd/dot_general | solution.py:115
  222.1 9.2 %convolution_convert_fusion.2 = bf16[768,3072]{1,0:T(8,128)(2,1)} fusion(bf16[576,3072]{1,0:T(8,128)(2,1)} %copy-done.50, f32[576,768]{1,0:T(8,128)} %fusion.20, f32[768]{0:T(1024)} %convert_element_type.311, f32[768]{0:T(1024)S(1)} %copy-done.38, f32[576]{0:T(1024)} %copy-done.39, f32[576]{0:T(1024)S(1)} %copy-done.33), kind=kOutput, calls=%fused_computation.23 | convolution fusion | flops 2722480128 | bytes 10037760 | tf_op jit(solution)/shard_map/iqd,iqf->df/dot_general | solution.py:119
  231.4 1.9 copy.88
  233.4 24.4 %reduce-scatter.15.cloned.1.call-done = bf16[768,576]{0,1:T(8,128)(2,1)} async-done(((bf16[768,2304]{0,1:T(8,128)(2,1)}), bf16[768,576]{0,1:T(8,128)(2,1)}) %reduce-scatter.15.cloned.1.call-update) | async-done | bytes 884752 | tf_op jit(solution)/shard_map/reduce_scatter | solution.py:31
  257.8 2.2 copy.86
  260.3 48.0 %reduce-scatter.23.cloned.1.call-done = bf16[3072,192]{0,1:T(8,128)(2,1)} async-done(((bf16[3072,768]{0,1:T(8,128)(2,1)}), bf16[3072,192]{0,1:T(8,128)(2,1)}) %reduce-scatter.23.cloned.1.call-update) | async-done | bytes 1179664 | tf_op jit(solution)/shard_map/reduce_scatter | solution.py:31
  308.3 2.5 copy.90
  310.8 6.8 %fusion.27 = bf16[1,576,768]{2,1,0:T(8,128)(2,1)S(1)} fusion(f32[576,768]{1,0:T(8,128)} %fusion.20, bf16[576,3072]{1,0:T(8,128)(2,1)} %get-tuple-element.114, bf16[3072,768]{1,0:T(8,128)(2,1)} %param.31, f32[768]{0:T(1024)S(1)} %convert_element_type.315, f32[576]{0:T(1024)S(1)} %convert_element_type.290), kind=kOutput, calls=%fused_computation.67 | convolution fusion | flops 2719678464 | bytes 10917120 | tf_op jit(solution)/shard_map/dot_general | solution.py:110
  317.6 2.6 copy.98
  320.8 8.0 %reduce.39 = bf16[576,768]{1,0:T(8,128)(2,1)} reduce(bf16[576,1,768]{2,1,0:T(2,128)(2,1)} %bitcast.134, bf16[]{:T(256)} %broadcast.353), dimensions={1}, to_apply=%bitcast.118.reduce_sub_computation | reduce | bytes 1769474
  328.8 3.5 reshape.788
  332.3 4.2 all-to-all-start.2
  336.8 6.8 %fusion.52 = (f32[768]{0:T(1024)S(1)}, f32[768]{0:T(1024)S(1)}, f32[576]{0:T(1024)S(1)}, f32[576]{0:T(1024)S(1)}, f32[576,768]{1,0:T(8,128)}) fusion(f32[576]{0:T(1024)S(1)} %copy-done.30, f32[576]{0:T(1024)S(1)} %copy-done.23, bf16[4,144,768]{2,1,0:T(8,128)(2,1)} %all-to-all-done.1, f32[576,768]{1,0:T(8,128)} %copy-done.15, ...), kind=kOutput, calls=%fused_computation.136 | convolution fusion | flops 2050815488 | bytes 10635264 | tf_op jit(solution)/shard_map/iqe,de->iqd/dot_general | solution.py:158
  348.6 19.5 %reduce-scatter.19.cloned.1.call-done = bf16[768,768]{1,0:T(8,128)(2,1)} async-done(((bf16[768,3072]{1,0:T(8,128)(2,1)}), bf16[768,768]{1,0:T(8,128)(2,1)}) %reduce-scatter.19.cloned.1.call-update) | async-done | bytes 1179664 | tf_op jit(solution)/shard_map/reduce_scatter | solution.py:31
  369.4 2.9 fusion.33
  373.6 2.6 copy.97
  376.2 7.9 %reduce.40 = bf16[576,768]{1,0:T(8,128)(2,1)} reduce(bf16[576,1,768]{2,1,0:T(2,128)(2,1)} %bitcast.135, bf16[]{:T(256)} %broadcast.353), dimensions={1}, to_apply=%bitcast.117.reduce_sub_computation | reduce | bytes 1769474
  384.1 3.4 reshape.790
  390.1 3.3 multiply_reduce_fusion.9
  394.0 4.5 all-to-all-start.4
  404.8 41.6 %psum.7 = f32[10752]{0:T(1024)} all-reduce(f32[10752]{0:T(1024)} %constant_dynamic-update-slice_fusion), channel_id=1, replica_groups=mesh['img'=8,'band'=4] {'img','band'}, use_global_device_ids=true, to_apply=%region_21.22 | all-reduce | flops 10752 | bytes 86016 | tf_op jit(solution)/shard_map/psum | solution.py:174
  458.0 3.8 reshape.789
  461.8 2.5 copy.92
  464.3 3.8 reshape.791
  468.2 2.5 copy.93
  472.2 7.9 %all_gather.13 = bf16[96,768]{0,1:T(8,128)(2,1)} all-gather(bf16[96,192]{0,1:T(8,128)(2,1)} %copy.89), channel_id=1, replica_groups=mesh['img'=8,'band'=4] {'band'}, dimensions={1}, use_global_device_ids=true | all-gather | bytes 184320 | tf_op jit(solution)/shard_map/all_gather | solution.py:33
  480.1 1.8 copy.80
  481.9 18.5 %reduce-scatter.25.cloned.1.call-done = bf16[96,576]{1,0:T(8,128)(2,1)} async-done(((bf16[768,576]{1,0:T(8,128)(2,1)}), bf16[96,576]{1,0:T(8,128)(2,1)}) %reduce-scatter.25.cloned.1.call-update) | async-done | bytes 110608
  502.1 1.7 copy.77
  503.8 7.2 %all-gather = bf16[4,576,96]{1,2,0:T(8,128)(2,1)S(1)} all-gather(bf16[1,576,96]{1,2,0:T(8,128)(2,1)} %copy.77), channel_id=1, replica_groups=mesh['img'=8,'band'=4] {'band'}, dimensions={0}, use_global_device_ids=true | all-gather | bytes 552960 | tf_op jit(solution)/shard_map/all_gather | solution.py:33
  512.2 2.7 reshape.779
  514.9 53.6 %reduce-scatter.29.cloned.1.call-done = bf16[384,192]{1,0:T(8,128)(2,1)} async-done(((bf16[3072,192]{1,0:T(8,128)(2,1)}), bf16[384,192]{1,0:T(8,128)(2,1)}) %reduce-scatter.29.cloned.1.call-update) | async-done | bytes 147472
  568.5 1.7 copy.91
  570.2 8.4 %all_gather.15 = bf16[384,768]{0,1:T(8,128)(2,1)} all-gather(bf16[384,192]{0,1:T(8,128)(2,1)} %copy.91), channel_id=1, replica_groups=mesh['img'=8,'band'=4] {'band'}, dimensions={1}, use_global_device_ids=true | all-gather | bytes 737280 | tf_op jit(solution)/shard_map/all_gather | solution.py:33
  578.5 2.3 copy.81
  580.8 54.7 %reduce-scatter.21.cloned.1.call-done = bf16[96,768]{1,0:T(8,128)(2,1)} async-done(((bf16[768,768]{1,0:T(8,128)(2,1)}), bf16[96,768]{1,0:T(8,128)(2,1)}) %reduce-scatter.21.cloned.1.call-update) | async-done | bytes 147472 | tf_op jit(solution)/shard_map/reduce_scatter | solution.py:32
  635.5 7.7 %all_gather.14 = bf16[96,3072]{1,0:T(8,128)(2,1)S(1)} all-gather(bf16[96,768]{1,0:T(8,128)(2,1)} %reduce-scatter.21.cloned.1.call-done), channel_id=1, replica_groups=mesh['img'=8,'band'=4] {'band'}, dimensions={1}, use_global_device_ids=true | all-gather | bytes 737280 | tf_op jit(solution)/shard_map/all_gather | solution.py:33
  (195 shorter events, 70.7 us)
Async XLA Ops:
  7.2 38.6 %copy-start = (bf16[768,2304]{1,0:T(8,128)(2,1)S(1)}, bf16[768,2304]{1,0:T(8,128)(2,1)}, u32[]{:S(2)}) copy-start(bf16[768,2304]{1,0:T(8,128)(2,1)} %param.22) | copy-start | bytes 10616836
  8.6 8.0 %all-to-all-start = ((s32[4,1,144]{2,1,0:T(1,128)}), s32[4,1,144]{2,1,0:T(1,128)S(1)}, u32[]{:S(2)}, u32[]{:S(2)}) async-start(s32[4,1,144]{2,1,0:T(1,128)} %all_to_all.17), calls=%async_computation | async-start | bytes 8192 | tf_op jit(solution)/shard_map/all_to_all | solution.py:66
  16.7 17.0 %all-to-all-start.1 = ((bf16[4,144,768]{2,1,0:T(8,128)(2,1)}), bf16[4,144,768]{2,1,0:T(8,128)(2,1)}, u32[]{:S(2)}, u32[]{:S(2)}) async-start(bf16[4,144,768]{2,1,0:T(8,128)(2,1)} %param.17), calls=%async_computation.1 | async-start | bytes 1769472 | tf_op jit(solution)/shard_map/all_to_all | solution.py:66
  33.7 88.0 %all-to-all-start.3 = ((bf16[4,144,768]{2,1,0:T(8,128)(2,1)}), bf16[4,144,768]{2,1,0:T(8,128)(2,1)}, u32[]{:S(2)}, u32[]{:S(2)}) async-start(bf16[4,144,768]{2,1,0:T(8,128)(2,1)} %param.33), calls=%async_computation.3 | async-start | bytes 1769472 | tf_op jit(solution)/shard_map/all_to_all | solution.py:66
  37.9 193.4 %reduce-scatter.17.cloned.1.call-start = ((), (), s32[]{:S(2)}) async-start(), calls=%async_computation.14 | async-start | bytes 1474560 | tf_op jit(solution)/shard_map/reduce_scatter | solution.py:31
  40.7 1.7 copy-start.22
  42.1 3.7 copy-start.34
  42.1 3.7 copy-start.41
  42.1 3.7 copy-start.42
  42.4 0.6 copy-start.29
  44.5 1.2 copy-start.15
  56.8 2.4 copy-start.21
  56.8 2.4 copy-start.24
  56.9 2.4 copy-start.25
  64.1 0.8 copy-start.2
  64.1 0.9 copy-start.4
  64.1 1.1 copy-start.6
  64.1 1.3 copy-start.8
  94.9 9.3 %copy-start.44 = (f32[768]{0:T(1024)S(1)}, f32[768]{0:T(1024)}, u32[]{:S(2)}) copy-start(f32[768]{0:T(1024)} %convert_element_type.309) | copy-start | bytes 9220
  94.9 9.3 %copy-start.47 = (bf16[768,768]{1,0:T(8,128)(2,1)S(1)}, bf16[768,768]{1,0:T(8,128)(2,1)}, u32[]{:S(2)}) copy-start(bf16[768,768]{1,0:T(8,128)(2,1)} %param.25) | copy-start | bytes 3538948
  103.3 0.9 copy-start.48
  110.4 1.8 copy-start.31
  112.3 0.6 copy-start.39
  123.1 9.2 %copy-start.20 = (bf16[576,768]{1,0:T(8,128)(2,1)}, bf16[576,768]{1,0:T(8,128)(2,1)S(1)}, u32[]{:S(2)}) copy-start(bf16[576,768]{1,0:T(8,128)(2,1)S(1)} %fusion.19) | copy-start | bytes 2654212
  123.1 9.2 %copy-start.1 = (f32[576,768]{1,0:T(8,128)S(1)}, f32[576,768]{1,0:T(8,128)}, u32[]{:S(2)}) copy-start(f32[576,768]{1,0:T(8,128)} %fusion.20) | copy-start | bytes 5308420
  123.1 9.2 %copy-start.32 = (f32[576]{0:T(1024)S(1)}, f32[576]{0:T(1024)}, u32[]{:S(2)}) copy-start(f32[576]{0:T(1024)} %copy-done.31) | copy-start | bytes 6916
  123.1 9.2 %copy-start.37 = (f32[768]{0:T(1024)S(1)}, f32[768]{0:T(1024)}, u32[]{:S(2)}) copy-start(f32[768]{0:T(1024)} %convert_element_type.310) | copy-start | bytes 9220
  123.2 9.2 %copy-start.40 = (f32[576]{0:T(1024)S(1)}, f32[576]{0:T(1024)}, u32[]{:S(2)}) copy-start(f32[576]{0:T(1024)} %copy-done.39) | copy-start | bytes 6916
  132.4 7.6 %copy-start.50 = (bf16[576,3072]{1,0:T(8,128)(2,1)}, bf16[576,3072]{1,0:T(8,128)(2,1)S(1)}, u32[]{:S(2)}) copy-start(bf16[576,3072]{1,0:T(8,128)(2,1)S(1)} %get-tuple-element.121) | copy-start | bytes 10616836
  140.0 3.8 copy-start.49
  142.6 1.2 copy-start.10
  151.8 15.5 %copy-start.27 = (f32[12,576]{1,0:T(8,128)S(1)}, f32[12,576]{1,0:T(8,128)}, u32[]{:S(2)}) copy-start(f32[12,576]{1,0:T(8,128)} %get-tuple-element.112) | copy-start | bytes 82948
  167.3 12.5 %copy-start.3 = (bf16[1,576,12,32]{1,3,2,0:T(8,128)(2,1)S(1)}, bf16[1,576,12,32]{1,3,2,0:T(8,128)(2,1)}, u32[]{:S(2)}) copy-start(bf16[1,576,12,32]{1,3,2,0:T(8,128)(2,1)} %copy-done.2) | copy-start | bytes 1327108
  167.3 12.6 %copy-start.5 = (bf16[1,576,12,32]{1,3,2,0:T(8,128)(2,1)S(1)}, bf16[1,576,12,32]{1,3,2,0:T(8,128)(2,1)}, u32[]{:S(2)}) copy-start(bf16[1,576,12,32]{1,3,2,0:T(8,128)(2,1)} %copy-done.4) | copy-start | bytes 1327108
  179.8 4.0 copy-start.7
  179.9 4.0 copy-start.9
  186.9 70.9 %reduce-scatter.15.cloned.1.call-start = ((), (), s32[]{:S(2)}) async-start(), calls=%async_computation.13 | async-start | bytes 4423680 | tf_op jit(solution)/shard_map/reduce_scatter | solution.py:31
  193.5 1.6 copy-start.17
  193.5 1.6 copy-start.28
  193.6 11.0 %copy-start.11 = (bf16[1,576,12,64]{1,3,2,0:T(8,128)(2,1)}, bf16[1,576,12,64]{1,3,2,0:T(8,128)(2,1)S(1)}, u32[]{:S(2)}) copy-start(bf16[1,576,12,64]{1,3,2,0:T(8,128)(2,1)S(1)} %maximum_convert_fusion) | copy-start | bytes 2654212
  195.1 9.5 %copy-start.13 = (bf16[1,576,12,64]{1,3,2,0:T(8,128)(2,1)}, bf16[1,576,12,64]{1,3,2,0:T(8,128)(2,1)S(1)}, u32[]{:S(2)}) copy-start(bf16[1,576,12,64]{1,3,2,0:T(8,128)(2,1)S(1)} %maximum_convert_fusion.1) | copy-start | bytes 2654212
  195.1 10.5 %copy-start.16 = (f32[576,768]{1,0:T(8,128)S(1)}, f32[576,768]{1,0:T(8,128)}, u32[]{:S(2)}) copy-start(f32[576,768]{1,0:T(8,128)} %copy-done.15) | copy-start | bytes 5308420
  195.1 10.5 %copy-start.35 = (f32[768]{0:T(1024)S(1)}, f32[768]{0:T(1024)}, u32[]{:S(2)}) copy-start(f32[768]{0:T(1024)} %convert_element_type.296) | copy-start | bytes 9220
  195.1 10.4 %copy-start.43 = (f32[768]{0:T(1024)S(1)}, f32[768]{0:T(1024)}, u32[]{:S(2)}) copy-start(f32[768]{0:T(1024)} %convert_element_type.297) | copy-start | bytes 9220
  204.6 0.9 copy-start.18
  212.8 95.5 %reduce-scatter.23.cloned.1.call-start = ((), (), s32[]{:S(2)}) async-start(), calls=%async_computation.17 | async-start | bytes 5898240 | tf_op jit(solution)/shard_map/reduce_scatter | solution.py:31
  221.3 0.7 copy-start.33
  221.3 0.7 copy-start.38
  221.4 146.7 %reduce-scatter.19.cloned.1.call-start = ((), (), s32[]{:S(2)}) async-start(), calls=%async_computation.15 | async-start | bytes 5898240 | tf_op jit(solution)/shard_map/reduce_scatter | solution.py:31
  231.3 29.0 %copy-start.46 = (bf16[768]{0:T(1024)(128)(2,1)S(1)}, bf16[768]{0:T(1024)(128)(2,1)}, u32[]{:S(2)}) copy-start(bf16[768]{0:T(1024)(128)(2,1)} %param.32) | copy-start | bytes 4612
  231.3 239.4 %reduce-scatter.27.cloned.1.call-start = ((), (), s32[]{:S(2)}) async-start(), calls=%async_computation.19 | async-start | bytes 442368
  233.3 267.1 %reduce-scatter.25.cloned.1.call-start = ((), (), s32[]{:S(2)}) async-start(), calls=%async_computation.18 | async-start | bytes 1105920
  260.0 308.4 %reduce-scatter.29.cloned.1.call-start = ((), (), s32[]{:S(2)}) async-start(), calls=%async_computation.20 | async-start | bytes 1769472
  328.8 8.0 %copy-start.23 = (f32[576]{0:T(1024)S(1)}, f32[576]{0:T(1024)}, u32[]{:S(2)}) copy-start(f32[576]{0:T(1024)} %copy-done.22) | copy-start | bytes 6916
  328.8 8.0 %copy-start.30 = (f32[576]{0:T(1024)S(1)}, f32[576]{0:T(1024)}, u32[]{:S(2)}) copy-start(f32[576]{0:T(1024)} %copy-done.29) | copy-start | bytes 6916
  332.3 61.7 %all-to-all-start.2 = ((bf16[4,2,55296]{2,1,0:T(2,128)(2,1)}), bf16[4,2,55296]{2,1,0:T(2,128)(2,1)}, u32[]{:S(2)}, u32[]{:S(2)}) async-start(bf16[4,2,55296]{2,1,0:T(2,128)(2,1)} %reshape.788), calls=%async_computation.2 | async-start | bytes 1769472 | tf_op jit(solution)/shard_map/all_to_all | solution.py:69
  336.5 299.0 %reduce-scatter.21.cloned.1.call-start = ((), (), s32[]{:S(2)}) async-start(), calls=%async_computation.16 | async-start | bytes 1327104 | tf_op jit(solution)/shard_map/reduce_scatter | solution.py:32
  336.8 9.4 %copy-start.12 = (bf16[1,576,12,64]{1,3,2,0:T(8,128)(2,1)S(1)}, bf16[1,576,12,64]{1,3,2,0:T(8,128)(2,1)}, u32[]{:S(2)}) copy-start(bf16[1,576,12,64]{1,3,2,0:T(8,128)(2,1)} %copy-done.11) | copy-start | bytes 2654212
  336.8 9.4 %copy-start.14 = (bf16[1,576,12,64]{1,3,2,0:T(8,128)(2,1)S(1)}, bf16[1,576,12,64]{1,3,2,0:T(8,128)(2,1)}, u32[]{:S(2)}) copy-start(bf16[1,576,12,64]{1,3,2,0:T(8,128)(2,1)} %copy-done.13) | copy-start | bytes 2654212
  336.8 9.4 %copy-start.19 = (bf16[12,64,576]{2,1,0:T(8,128)(2,1)S(1)}, bf16[12,64,576]{2,1,0:T(8,128)(2,1)}, u32[]{:S(2)}) copy-start(bf16[12,64,576]{2,1,0:T(8,128)(2,1)} %copy-done.18) | copy-start | bytes 2654212
  369.4 2.9 copy-start.36
  376.2 12.6 %copy-start.45 = (f32[768]{0:T(1024)S(1)}, f32[768]{0:T(1024)}, u32[]{:S(2)}) copy-start(f32[768]{0:T(1024)} %get-tuple-element.80) | copy-start | bytes 9220
  376.2 13.9 %copy-start.26 = (f32[576]{0:T(1024)S(1)}, f32[576]{0:T(1024)}, u32[]{:S(2)}) copy-start(f32[576]{0:T(1024)} %get-tuple-element.123) | copy-start | bytes 6916
  394.0 70.3 %all-to-all-start.4 = ((bf16[4,2,55296]{2,1,0:T(2,128)(2,1)}), bf16[4,2,55296]{2,1,0:T(2,128)(2,1)}, u32[]{:S(2)}, u32[]{:S(2)}) async-start(bf16[4,2,55296]{2,1,0:T(2,128)(2,1)} %reshape.790), calls=%async_computation.4 | async-start | bytes 1769472 | tf_op jit(solution)/shard_map/all_to_all | solution.py:69
Sparse Core Ops, SparseCore 0:
  187.0 27.7 reduce-scatter.16
  217.4 40.3 reduce-scatter.14
  260.3 47.9 reduce-scatter.22
  310.7 57.2 reduce-scatter.18
  371.1 62.2 reduce-scatter.26
  437.2 63.1 reduce-scatter.24
  503.8 64.5 reduce-scatter.28
  571.9 63.6 reduce-scatter.20
where the time goes:
time: 658 us; the launch traced here: 652 us
  waiting for transfers between devices  220 us (33%)
  matrix products  125 us (19%)
  other arithmetic  99.8 us (15%)
  local copies, waits for them, and re-layouts  95.8 us (15%)
  blocking collectives  72.8 us (11%)
  starting transfers between devices  22.4 us (3%)
  between operations  15.3 us (2%)
    reduce_scatter x4, waiting for transfers between devices, matrix_sum(): low = lax.psum_scatter(low, 'band', scatter_dimension=1, tiled=True)  91.9 us
    unnamed x11, waiting for transfers between devices  72.2 us
    unnamed x127, local copies, waits for them, and re-layouts  57.3 us
    reduce_scatter x1, waiting for transfers between devices, matrix_sum(): low = lax.psum_scatter(low, 'img', scatter_dimension=0, tiled=True)  54.7 us
    psum x1, blocking collectives, local(): packed = lax.psum(jnp.concatenate(small), ('img', 'band'))  41.6 us
    all_gather x4, blocking collectives, matrix_sum(): low = lax.all_gather(low, 'band', axis=1, tiled=True)  31.2 us
    sub x1, other arithmetic, local(): expo = jnp.exp(masked - jnp.max(masked, -1, keepdims=True))  22.2 us
    unnamed x3, other arithmetic  16 us
  transfers between devices with their start and end apart: 13, of which 7 were waited for; matrix products, arithmetic and copies ran while one was open for 38% of the time, Pallas kernels for 0%

commit v1 on v0

--- a/solution.py
+++ b/solution.py
@@ -8,6 +8,27 @@
 NEG = -1e30
 
 
+def collect(shard, axis, dim):
+    size, index, span = (lax.axis_size(axis), lax.axis_index(axis), shard.shape[dim])
+    ahead = [(i, (i + 1) % size) for i in range(size)]
+    left = [(i, (i - 1) % size) for i in range(size)]
+    out = jnp.zeros((*shard.shape[:dim], size * span, *shard.shape[dim + 1 :]), shard.dtype)
+    out = lax.dynamic_update_slice_in_dim(out, shard, index * span, axis=dim)
+    from_left = from_right = shard
+    middle = size // 2
+    for turn in range(1, middle + 1):
+        from_left = lax.ppermute(from_left, axis, ahead)
+        out = lax.dynamic_update_slice_in_dim(
+            out, from_left, (index - turn) % size * span, axis=dim
+        )
+        if turn < size - middle:
+            from_right = lax.ppermute(from_right, axis, left)
+            out = lax.dynamic_update_slice_in_dim(
+                out, from_right, (index + turn) % size * span, axis=dim
+            )
+    return out
+
+
 def norm_parts(values):
     center = values - jnp.mean(values, -1, keepdims=True)
     rstd = lax.rsqrt(jnp.mean(center * center, -1, keepdims=True) + EPS)
@@ -30,7 +51,7 @@
     low = grad.astype(jnp.bfloat16)
     low = lax.psum_scatter(low, "band", scatter_dimension=1, tiled=True)
     low = lax.psum_scatter(low, "img", scatter_dimension=0, tiled=True)
-    low = lax.all_gather(low, "band", axis=1, tiled=True)
+    low = collect(low, "band", 1)
     return low.astype(jnp.float32)
 
 

time: 658 us -> 736 us (1.12)
  waiting for transfers between devices: 220 us -> 272 us
  local copies, waits for them, and re-layouts: 95.8 us -> 137 us
  blocking collectives: 72.8 us -> 41.3 us
  other arithmetic: 99.8 us -> 109 us
  starting transfers between devices: 22.4 us -> 29.9 us
    reduce_scatter x1 -> x4, waiting for transfers between devices: 54.7 us -> 177 us  [matrix_sum(): low = lax.psum_scatter(low, 'img', scatter_dimension=0, tiled=True)]
    unnamed x11 -> x8, waiting for transfers between devices: 72.2 us -> 0.13 us
    dynamic_update_slice x0 -> x16, local copies, waits for them, and re-layouts: none -> 32.6 us  [the longest x8 16.2 us: collect(): lax.dynamic_update_slice_in_dim(out, from_left, (index - turn) % size * s...]
    all_gather x4 -> x0, blocking collectives: 31.2 us -> none  [matrix_sum(): low = lax.all_gather(low, 'band', axis=1, tiled=True)]
    ppermute x0 -> x9, local copies, waits for them, and re-layouts: none -> 14.8 us  [the longest x6 9.85 us: collect(): from_left = lax.ppermute(from_left, axis, ahead)]
    unnamed x127 -> x128, local copies, waits for them, and re-layouts: 57.3 us -> 51.3 us
  transfers between devices with their start and end apart: 13 -> 25, of which waited for: 7 -> 8; matrix products, arithmetic and copies ran while one was open for 38% -> 40% of each run, Pallas kernels for 0% -> 0%
where the time goes in v1:
time: 736 us; the launch traced here: 729 us
  waiting for transfers between devices  272 us (37%)
  local copies, waits for them, and re-layouts  137 us (19%)
  matrix products  125 us (17%)
  other arithmetic  109 us (15%)
  blocking collectives  41.3 us (6%)
  starting transfers between devices  29.9 us (4%)
  between operations  15.2 us (2%)
    reduce_scatter x4, waiting for transfers between devices, matrix_sum(): low = lax.psum_scatter(low, 'img', scatter_dimension=0, tiled=True)  177 us
    reduce_scatter x4, waiting for transfers between devices, matrix_sum(): low = lax.psum_scatter(low, 'band', scatter_dimension=1, tiled=True)  93.5 us
    unnamed x128, local copies, waits for them, and re-layouts  51.3 us
    psum x1, blocking collectives, local(): packed = lax.psum(jnp.concatenate(small), ('img', 'band'))  41.3 us
    sub x1, other arithmetic, local(): expo = jnp.exp(masked - jnp.max(masked, -1, keepdims=True))  22.2 us
    dynamic_update_slice x8, local copies, waits for them, and re-layouts, collect(): lax.dynamic_update_slice_in_dim(out, from_left, (index - turn) % size * s...  16.2 us
    unnamed x3, other arithmetic  15.9 us
    dot_general x1, matrix products, local(): jnp.einsum('iqhd,ikhd->ihqk', d_mix, value_low, preferred_element_type=si...  15.5 us
  transfers between devices with their start and end apart: 25, of which 8 were waited for; matrix products, arithmetic and copies ran while one was open for 40% of the time, Pallas kernels for 0%

profile of v1, /device:TPU:0, one launch (start us, length us, event | category | flops | bytes accessed | tf_op | source)
XLA Modules:
  0.0 728.7 jit_solution(13120359761600922291)
XLA Ops:
  8.6 4.2 all-to-all-start
  16.7 4.2 all-to-all-start.1
  33.7 4.2 all-to-all-start.3
  45.7 4.6 convolution_add_fusion
  50.3 6.6 copy.95
  56.9 2.4 slice_bitcast_fusion.1
  59.4 4.8 subtract_convert_fusion.1
  65.4 7.4 %fusion.34 = f32[12,576,576]{1,2,0:T(8,128)} fusion(bf16[576,12,32]{0,2,1:T(8,128)(2,1)S(1)} %bitcast.122, bf16[576,12,32]{0,2,1:T(8,128)(2,1)S(1)} %bitcast.124, bf16[576,12,32]{0,2,1:T(8,128)(2,1)S(1)} %bitcast.120, bf16[576,12,32]{0,2,1:T(8,128)(2,1)S(1)} %bitcast.118), kind=kOutput, calls=%fused_computation.88 | convolution fusion | flops 513146880 | bytes 17694720 | tf_op jit(solution)/shard_map/iqhd,ikhd->ihqk/dot_general | solution.py:114
  72.8 22.2 %fusion.55 = (f32[12,576]{1,0:T(8,128)}, f32[12,576,576]{1,2,0:T(8,128)}) fusion(f32[12,576,576]{1,2,0:T(8,128)} %fusion.34, pred[576]{0:T(1024)(128)(4,1)} %broadcast_compare_fusion), kind=kOutput, calls=%fused_computation.143 | output fusion | flops 23888448 | bytes 31878720 | tf_op jit(solution)/shard_map/sub | solution.py:116
  95.0 8.4 %fusion.21 = bf16[12,64,576]{2,1,0:T(8,128)(2,1)S(1)} fusion(f32[1,576,3,12,64]{1,4,3,2,0:T(8,128)} %bitcast.116, f32[12,576,576]{1,2,0:T(8,128)} %get-tuple-element.98, f32[12,576]{1,0:T(8,128)} %get-tuple-element.97), kind=kOutput, calls=%fused_computation.63 | convolution fusion | flops 518012928 | bytes 19603456 | tf_op jit(solution)/shard_map/ihqk,ikhd->iqhd/dot_general | solution.py:119
  104.3 3.3 fusion.20
  107.6 2.2 reduce_sum.183
  112.9 8.9 %multiply_convert_fusion.1 = (bf16[576,3072]{1,0:T(8,128)(2,1)}, f32[576,3072]{1,0:T(8,128)}) fusion(f32[3072]{0:T(1024)} %convert_element_type.313, bf16[768,3072]{1,0:T(8,128)(2,1)} %param.29, f32[576,768]{1,0:T(8,128)} %fusion.20, f32[768]{0:T(1024)} %convert_element_type.311, f32[768]{0:T(1024)} %convert_element_type.310, f32[576]{0:T(1024)S(1)} %add_rsqrt_fusion, ...), kind=kOutput, calls=%fused_computation.18 | convolution fusion | flops 2730737664 | bytes 17127936 | tf_op jit(solution)/shard_map/dot_general | solution.py:126
  123.3 9.3 %convert_reduce_fusion = (f32[3072]{0:T(1024)}, bf16[576,3072]{1,0:T(8,128)(2,1)S(1)}) fusion(f32[576,3072]{1,0:T(8,128)} %get-tuple-element.100, f32[3072]{0:T(1024)} %convert_element_type.313, bf16[576,768]{1,0:T(8,128)(2,1)S(1)} %fusion.19, bf16[3072,768]{1,0:T(8,128)(2,1)} %param.31), kind=kOutput, calls=%fused_computation.17 | convolution fusion | flops 2740909056 | bytes 16244736 | tf_op jit(solution)/shard_map/iqd,fd->iqf/dot_general | solution.py:138
  132.6 7.6 %multiply_reduce_fusion.1 = (f32[768]{0:T(1024)}, f32[576]{0:T(1024)S(1)}, f32[576]{0:T(1024)S(1)}, f32[768]{0:T(1024)}, f32[576,768]{1,0:T(8,128)S(1)}) fusion(f32[576,768]{1,0:T(8,128)S(1)} %copy-done.1, f32[576]{0:T(1024)S(1)} %copy-done.42, f32[576]{0:T(1024)S(1)} %copy-done.33, f32[768]{0:T(1024)S(1)} %copy-done.39, ...), kind=kOutput, calls=%fused_computation.46 | convolution fusion | flops 2721887744 | bytes 11814912 | tf_op jit(solution)/shard_map/iqf,df->iqd/dot_general | solution.py:142
  140.2 2.6 convert_reduce_fusion.2
  144.0 2.2 convolution_convert_fusion.3
  146.2 3.6 convolution_convert_fusion.4
  149.8 2.2 copy.99
  152.0 15.5 %multiply_reduce_fusion = (f32[12,576]{1,0:T(8,128)S(1)}, f32[12,576,576]{1,2,0:T(8,128)}) fusion(f32[12,576,576]{1,2,0:T(8,128)} %get-tuple-element.98, f32[12,576]{1,0:T(8,128)} %get-tuple-element.97, bf16[576,12,64]{0,2,1:T(8,128)(2,1)} %bitcast.138, f32[1,576,3,12,64]{1,4,3,2,0:T(8,128)} %bitcast.117), kind=kOutput, calls=%fused_computation.2 | convolution fusion | flops 521544960 | bytes 35654656 | tf_op jit(solution)/shard_map/iqhd,ikhd->ihqk/dot_general | solution.py:152
  167.5 12.2 %multiply_convert_fusion = bf16[12,576,576]{1,2,0:T(8,128)(2,1)S(1)} fusion(f32[12,576,576]{1,2,0:T(8,128)} %get-tuple-element.103, f32[12,576]{1,0:T(8,128)S(1)} %get-tuple-element.102, f32[12,576,576]{1,2,0:T(8,128)} %get-tuple-element.98, f32[12,576]{1,0:T(8,128)S(1)} %copy-done.28), kind=kLoop, calls=%fused_computation.1 | loop fusion | flops 15925248 | bytes 39868416 | tf_op jit(solution)/shard_map/convert_element_type | solution.py:154
  179.8 4.0 multiply_bitcast_fusion
  183.8 3.0 multiply_bitcast_fusion.1
  186.9 6.6 multiply_subtract_fusion.1
  195.1 9.5 %fusion.24 = bf16[12,64,576]{2,1,0:T(8,128)(2,1)S(1)} fusion(bf16[576,12,64]{0,2,1:T(8,128)(2,1)S(1)} %bitcast.139, f32[12,576,576]{1,2,0:T(8,128)} %get-tuple-element.98, f32[12,576]{1,0:T(8,128)S(1)} %copy-done.29), kind=kOutput, calls=%fused_computation.64 | convolution fusion | flops 518012928 | bytes 17722368 | tf_op jit(solution)/shard_map/ihqk,iqhd->ikhd/dot_general | solution.py:151
  205.5 7.3 convolution_convert_fusion
  213.1 8.3 %convolution_convert_fusion.1 = bf16[3072,768]{0,1:T(8,128)(2,1)} fusion(bf16[576,3072]{1,0:T(8,128)(2,1)} %get-tuple-element.99, bf16[576,768]{1,0:T(8,128)(2,1)} %copy-done.20), kind=kOutput, calls=%fused_computation.22 | convolution fusion | flops 2720268288 | bytes 9142272 | tf_op jit(solution)/shard_map/iqf,iqd->fd/dot_general | solution.py:136
  222.1 9.2 %convolution_convert_fusion.2 = bf16[768,3072]{1,0:T(8,128)(2,1)} fusion(bf16[576,3072]{1,0:T(8,128)(2,1)} %copy-done.52, f32[576,768]{1,0:T(8,128)} %fusion.20, f32[768]{0:T(1024)} %convert_element_type.311, f32[768]{0:T(1024)S(1)} %copy-done.40, f32[576]{0:T(1024)} %copy-done.41, f32[576]{0:T(1024)S(1)} %copy-done.34), kind=kOutput, calls=%fused_computation.23 | convolution fusion | flops 2722480128 | bytes 10037760 | tf_op jit(solution)/shard_map/iqd,iqf->df/dot_general | solution.py:140
  231.3 1.9 copy.123
  233.3 24.4 %reduce-scatter.15.cloned.1.call-done = bf16[768,576]{0,1:T(8,128)(2,1)} async-done(((bf16[768,2304]{0,1:T(8,128)(2,1)}), bf16[768,576]{0,1:T(8,128)(2,1)}) %reduce-scatter.15.cloned.1.call-update) | async-done | bytes 884752 | tf_op jit(solution)/shard_map/reduce_scatter | solution.py:52
  257.8 2.2 copy.121
  260.5 47.8 %reduce-scatter.23.cloned.1.call-done = bf16[3072,192]{0,1:T(8,128)(2,1)} async-done(((bf16[3072,768]{0,1:T(8,128)(2,1)}), bf16[3072,192]{0,1:T(8,128)(2,1)}) %reduce-scatter.23.cloned.1.call-update) | async-done | bytes 1179664 | tf_op jit(solution)/shard_map/reduce_scatter | solution.py:52
  308.3 2.5 copy.125
  311.0 6.8 fusion.27
  317.8 2.6 copy.133
  320.9 8.0 %reduce.39 = bf16[576,768]{1,0:T(8,128)(2,1)} reduce(bf16[576,1,768]{2,1,0:T(2,128)(2,1)} %bitcast.128, bf16[]{:T(256)} %broadcast.360), dimensions={1}, to_apply=%bitcast.112.reduce_sub_computation | reduce | bytes 1769474
  328.9 3.5 reshape.785
  332.4 4.3 all-to-all-start.2
  337.0 3.1 convert_reduce_fusion.1
  340.1 6.6 fusion.53
  346.7 21.3 %reduce-scatter.19.cloned.1.call-done = bf16[768,768]{1,0:T(8,128)(2,1)} async-done(((bf16[768,3072]{1,0:T(8,128)(2,1)}), bf16[768,768]{1,0:T(8,128)(2,1)}) %reduce-scatter.19.cloned.1.call-update) | async-done | bytes 1179664 | tf_op jit(solution)/shard_map/reduce_scatter | solution.py:52
  373.3 2.8 fusion.33
  377.5 2.6 copy.132
  380.1 7.9 %reduce.40 = bf16[576,768]{1,0:T(8,128)(2,1)} reduce(bf16[576,1,768]{2,1,0:T(2,128)(2,1)} %bitcast.129, bf16[]{:T(256)} %broadcast.360), dimensions={1}, to_apply=%bitcast.111.reduce_sub_computation | reduce | bytes 1769474
  388.0 3.4 reshape.787
  394.0 3.3 multiply_reduce_fusion.9
  397.9 4.4 all-to-all-start.4
  407.2 26.1 %reduce-scatter.27.cloned.1.call-done = bf16[96,192]{1,0:T(8,128)(2,1)} async-done(((bf16[768,192]{1,0:T(8,128)(2,1)}), bf16[96,192]{1,0:T(8,128)(2,1)}) %reduce-scatter.27.cloned.1.call-update) | async-done | bytes 36880 | tf_op jit(solution)/shard_map/reduce_scatter | solution.py:53
  436.6 63.6 %reduce-scatter.25.cloned.1.call-done = bf16[96,576]{1,0:T(8,128)(2,1)} async-done(((bf16[768,576]{1,0:T(8,128)(2,1)}), bf16[96,576]{1,0:T(8,128)(2,1)}) %reduce-scatter.25.cloned.1.call-update) | async-done | bytes 110608 | tf_op jit(solution)/shard_map/reduce_scatter | solution.py:53
  503.2 41.3 %psum.7 = f32[10752]{0:T(1024)} all-reduce(f32[10752]{0:T(1024)} %constant_dynamic-update-slice_fusion), channel_id=1, replica_groups=mesh['img'=8,'band'=4] {'img','band'}, use_global_device_ids=true, to_apply=%region_21.22 | all-reduce | flops 10752 | bytes 86016 | tf_op jit(solution)/shard_map/psum | solution.py:195
  546.9 21.6 %reduce-scatter.29.cloned.1.call-done = bf16[384,192]{1,0:T(8,128)(2,1)} async-done(((bf16[3072,192]{1,0:T(8,128)(2,1)}), bf16[384,192]{1,0:T(8,128)(2,1)}) %reduce-scatter.29.cloned.1.call-update) | async-done | bytes 147472 | tf_op jit(solution)/shard_map/reduce_scatter | solution.py:53
  570.2 65.4 %reduce-scatter.21.cloned.1.call-done = bf16[96,768]{1,0:T(8,128)(2,1)} async-done(((bf16[768,768]{1,0:T(8,128)(2,1)}), bf16[96,768]{1,0:T(8,128)(2,1)}) %reduce-scatter.21.cloned.1.call-update) | async-done | bytes 147472 | tf_op jit(solution)/shard_map/reduce_scatter | solution.py:53
  647.2 3.8 reshape.786
  651.0 2.5 copy.127
  653.5 3.8 reshape.788
  657.3 2.5 copy.128
  680.8 2.1 dynamic_update_slice.50
  686.3 2.0 convert_element_type.337
  692.5 3.3 dynamic_update_slice.60
  700.6 3.1 dynamic_update_slice.61
  705.4 3.7 dynamic_update_slice.62
  712.4 3.3 dynamic_update_slice.63
  715.7 2.2 convert_element_type.343
  719.4 2.2 convert_element_type.341
  (246 shorter events, 115.1 us)
Async XLA Ops:
  7.2 38.5 %copy-start = (bf16[768,2304]{1,0:T(8,128)(2,1)S(1)}, bf16[768,2304]{1,0:T(8,128)(2,1)}, u32[]{:S(2)}) copy-start(bf16[768,2304]{1,0:T(8,128)(2,1)} %param.22) | copy-start | bytes 10616836
  8.6 8.0 %all-to-all-start = ((s32[4,1,144]{2,1,0:T(1,128)}), s32[4,1,144]{2,1,0:T(1,128)S(1)}, u32[]{:S(2)}, u32[]{:S(2)}) async-start(s32[4,1,144]{2,1,0:T(1,128)} %all_to_all.17), calls=%async_computation | async-start | bytes 8192 | tf_op jit(solution)/shard_map/all_to_all | solution.py:87
  16.7 17.0 %all-to-all-start.1 = ((bf16[4,144,768]{2,1,0:T(8,128)(2,1)}), bf16[4,144,768]{2,1,0:T(8,128)(2,1)}, u32[]{:S(2)}, u32[]{:S(2)}) async-start(bf16[4,144,768]{2,1,0:T(8,128)(2,1)} %param.17), calls=%async_computation.1 | async-start | bytes 1769472 | tf_op jit(solution)/shard_map/all_to_all | solution.py:87
  33.7 88.2 %all-to-all-start.3 = ((bf16[4,144,768]{2,1,0:T(8,128)(2,1)}), bf16[4,144,768]{2,1,0:T(8,128)(2,1)}, u32[]{:S(2)}, u32[]{:S(2)}) async-start(bf16[4,144,768]{2,1,0:T(8,128)(2,1)} %param.33), calls=%async_computation.3 | async-start | bytes 1769472 | tf_op jit(solution)/shard_map/all_to_all | solution.py:87
  37.9 193.4 %reduce-scatter.17.cloned.1.call-start = ((), (), s32[]{:S(2)}) async-start(), calls=%async_computation.14 | async-start | bytes 1474560 | tf_op jit(solution)/shard_map/reduce_scatter | solution.py:52
  40.7 1.7 copy-start.23
  42.0 3.7 copy-start.35
  42.1 3.7 copy-start.43
  42.1 3.6 copy-start.44
  56.9 2.4 copy-start.22
  56.9 2.4 copy-start.25
  56.9 2.4 copy-start.26
  95.0 9.3 %copy-start.46 = (f32[768]{0:T(1024)S(1)}, f32[768]{0:T(1024)}, u32[]{:S(2)}) copy-start(f32[768]{0:T(1024)} %convert_element_type.309) | copy-start | bytes 9220
  95.0 9.3 %copy-start.49 = (bf16[768,768]{1,0:T(8,128)(2,1)S(1)}, bf16[768,768]{1,0:T(8,128)(2,1)}, u32[]{:S(2)}) copy-start(bf16[768,768]{1,0:T(8,128)(2,1)} %param.25) | copy-start | bytes 3538948
  110.5 1.8 copy-start.32
  123.2 9.3 %copy-start.20 = (bf16[576,768]{1,0:T(8,128)(2,1)}, bf16[576,768]{1,0:T(8,128)(2,1)S(1)}, u32[]{:S(2)}) copy-start(bf16[576,768]{1,0:T(8,128)(2,1)S(1)} %fusion.19) | copy-start | bytes 2654212
  123.3 9.3 %copy-start.1 = (f32[576,768]{1,0:T(8,128)S(1)}, f32[576,768]{1,0:T(8,128)}, u32[]{:S(2)}) copy-start(f32[576,768]{1,0:T(8,128)} %fusion.20) | copy-start | bytes 5308420
  123.3 9.3 %copy-start.33 = (f32[576]{0:T(1024)S(1)}, f32[576]{0:T(1024)}, u32[]{:S(2)}) copy-start(f32[576]{0:T(1024)} %copy-done.32) | copy-start | bytes 6916
  123.3 9.3 %copy-start.39 = (f32[768]{0:T(1024)S(1)}, f32[768]{0:T(1024)}, u32[]{:S(2)}) copy-start(f32[768]{0:T(1024)} %convert_element_type.310) | copy-start | bytes 9220
  123.3 9.3 %copy-start.42 = (f32[576]{0:T(1024)S(1)}, f32[576]{0:T(1024)}, u32[]{:S(2)}) copy-start(f32[576]{0:T(1024)} %copy-done.41) | copy-start | bytes 6916
  132.6 7.6 %copy-start.52 = (bf16[576,3072]{1,0:T(8,128)(2,1)}, bf16[576,3072]{1,0:T(8,128)(2,1)S(1)}, u32[]{:S(2)}) copy-start(bf16[576,3072]{1,0:T(8,128)(2,1)S(1)} %get-tuple-element.106) | copy-start | bytes 10616836
  140.2 3.8 copy-start.51
  152.0 15.5 %copy-start.28 = (f32[12,576]{1,0:T(8,128)S(1)}, f32[12,576]{1,0:T(8,128)}, u32[]{:S(2)}) copy-start(f32[12,576]{1,0:T(8,128)} %get-tuple-element.97) | copy-start | bytes 82948
  167.5 12.3 %copy-start.3 = (bf16[1,576,12,32]{1,3,2,0:T(8,128)(2,1)S(1)}, bf16[1,576,12,32]{1,3,2,0:T(8,128)(2,1)}, u32[]{:S(2)}) copy-start(bf16[1,576,12,32]{1,3,2,0:T(8,128)(2,1)} %copy-done.2) | copy-start | bytes 1327108
  167.5 12.3 %copy-start.5 = (bf16[1,576,12,32]{1,3,2,0:T(8,128)(2,1)S(1)}, bf16[1,576,12,32]{1,3,2,0:T(8,128)(2,1)}, u32[]{:S(2)}) copy-start(bf16[1,576,12,32]{1,3,2,0:T(8,128)(2,1)} %copy-done.4) | copy-start | bytes 1327108
  179.8 4.0 copy-start.7
  179.8 4.0 copy-start.9
  186.8 70.9 %reduce-scatter.15.cloned.1.call-start = ((), (), s32[]{:S(2)}) async-start(), calls=%async_computation.13 | async-start | bytes 4423680 | tf_op jit(solution)/shard_map/reduce_scatter | solution.py:52
  193.6 11.0 %copy-start.11 = (bf16[1,576,12,64]{1,3,2,0:T(8,128)(2,1)}, bf16[1,576,12,64]{1,3,2,0:T(8,128)(2,1)S(1)}, u32[]{:S(2)}) copy-start(bf16[1,576,12,64]{1,3,2,0:T(8,128)(2,1)S(1)} %maximum_convert_fusion) | copy-start | bytes 2654212
  195.1 9.5 %copy-start.13 = (bf16[1,576,12,64]{1,3,2,0:T(8,128)(2,1)}, bf16[1,576,12,64]{1,3,2,0:T(8,128)(2,1)S(1)}, u32[]{:S(2)}) copy-start(bf16[1,576,12,64]{1,3,2,0:T(8,128)(2,1)S(1)} %maximum_convert_fusion.1) | copy-start | bytes 2654212
  195.1 10.5 %copy-start.16 = (f32[576,768]{1,0:T(8,128)S(1)}, f32[576,768]{1,0:T(8,128)}, u32[]{:S(2)}) copy-start(f32[576,768]{1,0:T(8,128)} %copy-done.15) | copy-start | bytes 5308420
  195.1 10.5 %copy-start.36 = (f32[768]{0:T(1024)S(1)}, f32[768]{0:T(1024)}, u32[]{:S(2)}) copy-start(f32[768]{0:T(1024)} %convert_element_type.296) | copy-start | bytes 9220
  195.1 10.5 %copy-start.45 = (f32[768]{0:T(1024)S(1)}, f32[768]{0:T(1024)}, u32[]{:S(2)}) copy-start(f32[768]{0:T(1024)} %convert_element_type.297) | copy-start | bytes 9220
  212.8 95.5 %reduce-scatter.23.cloned.1.call-start = ((), (), s32[]{:S(2)}) async-start(), calls=%async_computation.17 | async-start | bytes 5898240 | tf_op jit(solution)/shard_map/reduce_scatter | solution.py:52
  221.4 146.6 %reduce-scatter.19.cloned.1.call-start = ((), (), s32[]{:S(2)}) async-start(), calls=%async_computation.15 | async-start | bytes 5898240 | tf_op jit(solution)/shard_map/reduce_scatter | solution.py:52
  231.3 202.1 %reduce-scatter.27.cloned.1.call-start = ((), (), s32[]{:S(2)}) async-start(), calls=%async_computation.19 | async-start | bytes 442368 | tf_op jit(solution)/shard_map/reduce_scatter | solution.py:53
  233.3 267.0 %reduce-scatter.25.cloned.1.call-start = ((), (), s32[]{:S(2)}) async-start(), calls=%async_computation.18 | async-start | bytes 1105920 | tf_op jit(solution)/shard_map/reduce_scatter | solution.py:53
  260.0 50.9 %copy-start.48 = (bf16[768]{0:T(1024)(128)(2,1)S(1)}, bf16[768]{0:T(1024)(128)(2,1)}, u32[]{:S(2)}) copy-start(bf16[768]{0:T(1024)(128)(2,1)} %param.32) | copy-start | bytes 4612
  260.0 308.5 %reduce-scatter.29.cloned.1.call-start = ((), (), s32[]{:S(2)}) async-start(), calls=%async_computation.20 | async-start | bytes 1769472 | tf_op jit(solution)/shard_map/reduce_scatter | solution.py:53
  332.4 7.7 %copy-start.24 = (f32[576]{0:T(1024)S(1)}, f32[576]{0:T(1024)}, u32[]{:S(2)}) copy-start(f32[576]{0:T(1024)} %copy-done.23) | copy-start | bytes 6916
  332.4 7.7 %copy-start.31 = (f32[576]{0:T(1024)S(1)}, f32[576]{0:T(1024)}, u32[]{:S(2)}) copy-start(f32[576]{0:T(1024)} %copy-done.30) | copy-start | bytes 6916
  332.4 65.4 %all-to-all-start.2 = ((bf16[4,2,55296]{2,1,0:T(2,128)(2,1)}), bf16[4,2,55296]{2,1,0:T(2,128)(2,1)}, u32[]{:S(2)}, u32[]{:S(2)}) async-start(bf16[4,2,55296]{2,1,0:T(2,128)(2,1)} %reshape.785), calls=%async_computation.2 | async-start | bytes 1769472 | tf_op jit(solution)/shard_map/all_to_all | solution.py:90
  336.8 298.8 %reduce-scatter.21.cloned.1.call-start = ((), (), s32[]{:S(2)}) async-start(), calls=%async_computation.16 | async-start | bytes 1327104 | tf_op jit(solution)/shard_map/reduce_scatter | solution.py:53
  337.0 3.1 copy-start.12
  337.0 3.1 copy-start.14
  337.0 3.1 copy-start.19
  337.0 3.1 copy-start.37
  373.3 2.9 copy-start.38
  380.1 12.6 %copy-start.47 = (f32[768]{0:T(1024)S(1)}, f32[768]{0:T(1024)}, u32[]{:S(2)}) copy-start(f32[768]{0:T(1024)} %get-tuple-element.65) | copy-start | bytes 9220
  380.1 13.9 %copy-start.27 = (f32[576]{0:T(1024)S(1)}, f32[576]{0:T(1024)}, u32[]{:S(2)}) copy-start(f32[576]{0:T(1024)} %get-tuple-element.108) | copy-start | bytes 6916
  397.9 255.6 %all-to-all-start.4 = ((bf16[4,2,55296]{2,1,0:T(2,128)(2,1)}), bf16[4,2,55296]{2,1,0:T(2,128)(2,1)}, u32[]{:S(2)}, u32[]{:S(2)}) async-start(bf16[4,2,55296]{2,1,0:T(2,128)(2,1)} %reshape.787), calls=%async_computation.4 | async-start | bytes 1769472 | tf_op jit(solution)/shard_map/all_to_all | solution.py:90
  434.9 109.6 %collective-permute-start.3 = (bf16[96,192]{0,1:T(8,128)(2,1)}, bf16[96,192]{0,1:T(8,128)(2,1)}, u32[]{:S(2)}, u32[]{:S(2)}) collective-permute-start(bf16[96,192]{0,1:T(8,128)(2,1)} %copy.124), channel_id=1, source_target_pairs={{0,1},{1,2},{2,3},{3,0},{4,5},{5,6},{6,7},{7,4},{8,9},{9,10},{10,1... | collective-permute-start | bytes 110600 | tf_op jit(solution)/shard_map/ppermute | solution.py:20
  434.9 135.4 %collective-permute-start.4 = (bf16[96,192]{0,1:T(8,128)(2,1)}, bf16[96,192]{0,1:T(8,128)(2,1)}, u32[]{:S(2)}, u32[]{:S(2)}) collective-permute-start(bf16[96,192]{0,1:T(8,128)(2,1)} %copy.124), channel_id=1, source_target_pairs={{0,3},{1,0},{2,1},{3,2},{4,7},{5,4},{6,5},{7,6},{8,11},{9,8},{10,9... | collective-permute-start | bytes 110600 | tf_op jit(solution)/shard_map/ppermute | solution.py:25
  501.9 44.3 %collective-permute-start = (bf16[96,576]{0,1:T(8,128)(2,1)}, bf16[96,576]{0,1:T(8,128)(2,1)}, u32[]{:S(2)}, u32[]{:S(2)}) collective-permute-start(bf16[96,576]{0,1:T(8,128)(2,1)} %copy.122), channel_id=1, source_target_pairs={{0,1},{1,2},{2,3},{3,0},{4,5},{5,6},{6,7},{7,4},{8,9},{9,10},{10,1... | collective-permute-start | bytes 331784 | tf_op jit(solution)/shard_map/ppermute | solution.py:20
  544.5 123.9 %collective-permute-start.5 = (bf16[96,192]{0,1:T(8,128)(2,1)}, bf16[96,192]{0,1:T(8,128)(2,1)}, u32[]{:S(2)}, u32[]{:S(2)}) collective-permute-start(bf16[96,192]{0,1:T(8,128)(2,1)} %collective-permute-done.3), channel_id=1, source_target_pairs={{0,1},{1,2},{2,3},{3,0},{4,5},{5,6},{6,7},{7,4},{8,9},{9,10},{10,1... | collective-permute-start | bytes 110600 | tf_op jit(solution)/shard_map/ppermute | solution.py:20
  544.5 134.6 %collective-permute-start.1 = (bf16[96,576]{0,1:T(8,128)(2,1)}, bf16[96,576]{0,1:T(8,128)(2,1)}, u32[]{:S(2)}, u32[]{:S(2)}) collective-permute-start(bf16[96,576]{0,1:T(8,128)(2,1)} %copy.122), channel_id=1, source_target_pairs={{0,3},{1,0},{2,1},{3,2},{4,7},{5,4},{6,5},{7,6},{8,11},{9,8},{10,9... | collective-permute-start | bytes 331784 | tf_op jit(solution)/shard_map/ppermute | solution.py:25
  546.2 136.6 %collective-permute-start.2 = (bf16[96,576]{0,1:T(8,128)(2,1)}, bf16[96,576]{0,1:T(8,128)(2,1)}, u32[]{:S(2)}, u32[]{:S(2)}) collective-permute-start(bf16[96,576]{0,1:T(8,128)(2,1)} %collective-permute-done), channel_id=1, source_target_pairs={{0,1},{1,2},{2,3},{3,0},{4,5},{5,6},{6,7},{7,4},{8,9},{9,10},{10,1... | collective-permute-start | bytes 331784 | tf_op jit(solution)/shard_map/ppermute | solution.py:20
  570.2 125.6 %collective-permute-start.9 = (bf16[384,192]{0,1:T(8,128)(2,1)}, bf16[384,192]{0,1:T(8,128)(2,1)}, u32[]{:S(2)}, u32[]{:S(2)}) collective-permute-start(bf16[384,192]{0,1:T(8,128)(2,1)} %copy.126), channel_id=1, source_target_pairs={{0,1},{1,2},{2,3},{3,0},{4,5},{5,6},{6,7},{7,4},{8,9},{9,10},{10,1... | collective-permute-start | bytes 442376 | tf_op jit(solution)/shard_map/ppermute | solution.py:20
  635.6 61.1 %collective-permute-start.6 = (bf16[96,768]{1,0:T(8,128)(2,1)}, bf16[96,768]{1,0:T(8,128)(2,1)}, u32[]{:S(2)}, u32[]{:S(2)}) collective-permute-start(bf16[96,768]{1,0:T(8,128)(2,1)} %reduce-scatter.21.cloned.1.call-done), channel_id=1, source_target_pairs={{0,1},{1,2},{2,3},{3,0},{4,5},{5,6},{6,7},{7,4},{8,9},{9,10},{10,1... | collective-permute-start | bytes 442376 | tf_op jit(solution)/shard_map/ppermute | solution.py:20
  686.3 4.7 copy-start.21
  688.3 15.4 %collective-permute-start.10 = (bf16[384,192]{0,1:T(8,128)(2,1)}, bf16[384,192]{0,1:T(8,128)(2,1)}, u32[]{:S(2)}, u32[]{:S(2)}) collective-permute-start(bf16[384,192]{0,1:T(8,128)(2,1)} %copy.126), channel_id=1, source_target_pairs={{0,3},{1,0},{2,1},{3,2},{4,7},{5,4},{6,5},{7,6},{8,11},{9,8},{10,9... | collective-permute-start | bytes 442376 | tf_op jit(solution)/shard_map/ppermute | solution.py:25
  690.1 19.0 %collective-permute-start.7 = (bf16[96,768]{1,0:T(8,128)(2,1)}, bf16[96,768]{1,0:T(8,128)(2,1)}, u32[]{:S(2)}, u32[]{:S(2)}) collective-permute-start(bf16[96,768]{1,0:T(8,128)(2,1)} %reduce-scatter.21.cloned.1.call-done), channel_id=1, source_target_pairs={{0,3},{1,0},{2,1},{3,2},{4,7},{5,4},{6,5},{7,6},{8,11},{9,8},{10,9... | collective-permute-start | bytes 442376 | tf_op jit(solution)/shard_map/ppermute | solution.py:25
  695.8 14.9 %collective-permute-start.11 = (bf16[384,192]{0,1:T(8,128)(2,1)}, bf16[384,192]{0,1:T(8,128)(2,1)}, u32[]{:S(2)}, u32[]{:S(2)}) collective-permute-start(bf16[384,192]{0,1:T(8,128)(2,1)} %collective-permute-done.9), channel_id=1, source_target_pairs={{0,1},{1,2},{2,3},{3,0},{4,5},{5,6},{6,7},{7,4},{8,9},{9,10},{10,1... | collective-permute-start | bytes 442376 | tf_op jit(solution)/shard_map/ppermute | solution.py:20
  696.7 21.2 %collective-permute-start.8 = (bf16[96,768]{1,0:T(8,128)(2,1)}, bf16[96,768]{1,0:T(8,128)(2,1)}, u32[]{:S(2)}, u32[]{:S(2)}) collective-permute-start(bf16[96,768]{1,0:T(8,128)(2,1)} %collective-permute-done.6), channel_id=1, source_target_pairs={{0,1},{1,2},{2,3},{3,0},{4,5},{5,6},{6,7},{7,4},{8,9},{9,10},{10,1... | collective-permute-start | bytes 442376 | tf_op jit(solution)/shard_map/ppermute | solution.py:20
  (14 other events, 14.1 us)
Sparse Core Ops, SparseCore 0:
  186.9 27.8 reduce-scatter.16
  217.4 40.3 reduce-scatter.14
  260.3 47.9 reduce-scatter.22
  310.7 57.2 reduce-scatter.18
  371.1 62.1 reduce-scatter.26
  437.1 63.0 reduce-scatter.24
  503.7 64.8 reduce-scatter.28
  571.9 63.6 reduce-scatter.20
